TPU v7x, 32 devices: a whole 2x2x4 slice. The times are simulated.
32 devices in a mesh: groups: 2 (over y), expert: 4 (over z), dp: 2 (over x), inner: 2 (over core).
Axes of the slice: x: 2, y: 2, z: 4, core: 2. Of those that a mesh axis runs over, the one named last changes fastest.
Arguments:
- tokens: bfloat16 [2048, 1536], P(('groups', 'expert', 'dp'), 'inner'), parts along dimension 0, may hold values from -6 to 6
- out_grad: bfloat16 [2048, 1536], P(('groups', 'expert', 'dp'), 'inner'), parts along dimension 0, may hold values from -6 to 6
- expert_ids: int32 [2048, 8], P(('groups', 'expert', 'dp')), parts along dimension 0, may hold values from 0 to 63, all different within a row; in each aligned block of 128 rows (0 to 127, 128 to 255, ...) at most 17 rows name the same one
- gate_probs: float32 [2048, 8], P(('groups', 'expert', 'dp')), parts along dimension 0, may hold values from 0.05 to 0.5
- gate_weight: bfloat16 [64, 1536, 384], P('expert', 'inner', 'dp'), may hold values from -0.15625 to 0.15625
- up_weight: bfloat16 [64, 1536, 384], P('expert', 'inner', 'dp'), may hold values from -0.15625 to 0.15625
- down_weight: bfloat16 [64, 384, 1536], P('expert', 'dp', 'inner'), may hold values from -0.3125 to 0.3125
Outputs:
- token_grad: bfloat16 [2048, 1536], P(('groups', 'expert', 'dp'), 'inner'), parts along dimension 0
- prob_grad: float32 [2048, 8], P(('groups', 'expert', 'dp')), parts along dimension 0
- gate_weight_grad: bfloat16 [128, 1536, 384], P(('groups', 'expert'), 'inner', 'dp'), parts along dimension 0
- up_weight_grad: bfloat16 [128, 1536, 384], P(('groups', 'expert'), 'inner', 'dp'), parts along dimension 0
- down_weight_grad: bfloat16 [128, 384, 1536], P(('groups', 'expert'), 'dp', 'inner'), parts along dimension 0
There are 2 independent parts, one for each index of `groups`. A program takes and returns all parts, laid end to end along the dimension named above; an argument that names none is the same for every part. Nothing has to cross between parts.
Inputs may be any that keep to these rules, and one draw needn't show every extreme that they name: `expert_ids`: within the rows of one block of 128 tokens no expert is chosen more than 17 times, and some expert is chosen exactly 17 times in some block; a token's 8 experts differ.
All inputs are finite; a program needn't handle non-finite values.
Results may differ from a plain program's by a relative error of at most 0.015.
Values may be sent and summed in bfloat16 or wider, within the bound.
A program may use at most 192 MiB of HBM per device.

v0:
```python
import jax
import jax.numpy as jnp
from jax import lax
from jax.sharding import PartitionSpec as P

F32 = jnp.float32
BF16 = jnp.bfloat16


def select_rows(packed, width, top_count, per_dev, block_rows, capacity):
    total = packed.shape[0]
    blocks = total // block_rows
    run = 4 if blocks % 4 == 0 else 1
    runs = blocks // run
    span = run * block_rows
    rows = -(-run * capacity // 16) * 16
    ids = packed[:, 2 * width : 2 * width + top_count].astype(jnp.int32)
    probs = packed[:, 2 * width + top_count : 2 * width + 2 * top_count]
    mine = lax.axis_index("expert") * per_dev + jnp.arange(per_dev, dtype=jnp.int32)
    hits = ids[:, :, None] == mine[None, None, :]
    member = jnp.any(hits, axis=1).reshape(runs, span, per_dev)
    weight = jnp.sum(jnp.where(hits, probs[:, :, None].astype(F32), 0.0), axis=1)
    weight = weight.reshape(runs, span, per_dev)
    at = jnp.arange(span, dtype=jnp.int32)
    earlier = (at[:, None] > at[None, :]).astype(BF16)
    slot = jnp.einsum("ts,gse->get", earlier, member.astype(BF16), preferred_element_type=F32)
    slot = jnp.where(member.transpose(0, 2, 1), slot.astype(jnp.int32), -1)
    places = jnp.arange(rows, dtype=jnp.int32)
    picked = slot[:, :, None, :] == places[None, None, :, None]
    row_prob = jnp.sum(jnp.where(picked, weight.transpose(0, 2, 1)[:, :, None, :], 0.0), axis=3)
    return (picked.astype(BF16), row_prob, hits, runs, span, rows)


def on_device(tokens, out_grad, expert_ids, gate_probs, gate_weight, up_weight, down_weight):
    tok_rows, width = tokens.shape
    top_count = expert_ids.shape[1]
    per_dev = gate_weight.shape[0]
    experts = per_dev * lax.axis_size("expert")
    capacity = tok_rows * top_count // experts + 1
    packed = jnp.concatenate(
        [tokens, out_grad, expert_ids.astype(BF16), gate_probs.astype(BF16)], axis=1
    )
    packed = lax.all_gather(packed, ("expert", "dp"), axis=0, tiled=True)
    picked, row_prob, hits, runs, span, rows = select_rows(
        packed, width, top_count, per_dev, tok_rows, capacity
    )
    both = packed[:, : 2 * width].reshape(runs, span, 2 * width)
    sorted_rows = jnp.einsum("gest,gtd->egsd", picked, both, preferred_element_type=F32)
    sorted_rows = sorted_rows.astype(BF16).reshape(per_dev, runs * rows, 2 * width)
    expert_rows, expert_grads = (sorted_rows[:, :, :width], sorted_rows[:, :, width:])
    prob_col = row_prob.transpose(1, 0, 2).reshape(per_dev, runs * rows, 1)
    hid = gate_weight.shape[2]
    parts = jnp.concatenate(
        [
            jnp.einsum("jrd,jdf->jrf", expert_rows, gate_weight, preferred_element_type=F32),
            jnp.einsum("jrd,jdf->jrf", expert_rows, up_weight, preferred_element_type=F32),
            jnp.einsum("jrd,jfd->jrf", expert_grads, down_weight, preferred_element_type=F32),
        ],
        axis=2,
    ).astype(BF16)
    sums = lax.psum(parts, "inner").astype(F32)
    gate, up, slope = (sums[..., :hid], sums[..., hid : 2 * hid], sums[..., 2 * hid :])
    sig = jax.nn.sigmoid(gate)
    act = gate * sig
    hidden = (act * up).astype(BF16)
    scores = jnp.sum(hidden.astype(F32) * slope, axis=-1)
    hidden_grad = prob_col * slope
    gate_back = (hidden_grad * up * sig * (1.0 + gate * (1.0 - sig))).astype(BF16)
    up_back = (hidden_grad * act).astype(BF16)
    row_grads = jnp.einsum("jrf,jdf->jrd", gate_back, gate_weight, preferred_element_type=F32)
    row_grads = (
        row_grads + jnp.einsum("jrf,jdf->jrd", up_back, up_weight, preferred_element_type=F32)
    ).astype(BF16)
    token_part = jnp.einsum(
        "gest,egsd->gtd",
        picked,
        row_grads.reshape(per_dev, runs, rows, width),
        preferred_element_type=F32,
    ).reshape(runs * span, width)
    score_rows = scores.reshape(per_dev, runs, rows).transpose(1, 0, 2)
    score_part = jnp.sum(picked.astype(F32) * score_rows[..., None], axis=2)
    score_part = score_part.transpose(0, 2, 1).reshape(runs * span, 1, per_dev)
    score_part = jnp.sum(jnp.where(hits, score_part, 0.0), axis=2)
    returned = lax.psum_scatter(
        jnp.concatenate([token_part, score_part], axis=1).astype(BF16),
        ("expert", "dp"),
        scatter_dimension=0,
        tiled=True,
    )
    grad_gate = jnp.einsum("jrd,jrf->jdf", expert_rows, gate_back, preferred_element_type=F32)
    grad_up = jnp.einsum("jrd,jrf->jdf", expert_rows, up_back, preferred_element_type=F32)
    down_rows = (prob_col * expert_grads.astype(F32)).astype(BF16)
    grad_down = jnp.einsum("jrf,jrd->jfd", hidden, down_rows, preferred_element_type=F32)
    return (
        returned[:, :width],
        returned[:, width:].astype(F32),
        grad_gate.astype(BF16),
        grad_up.astype(BF16),
        grad_down.astype(BF16),
    )


def solution(mesh):
    placed = (
        P(("groups", "expert", "dp"), "inner"),
        P(("groups", "expert", "dp"), "inner"),
        P(("groups", "expert", "dp"), None),
        P(("groups", "expert", "dp"), None),
        P("expert", "inner", "dp"),
        P("expert", "inner", "dp"),
        P("expert", "dp", "inner"),
    )
    return jax.shard_map(
        on_device,
        mesh=mesh,
        in_specs=placed,
        out_specs=(
            P(("groups", "expert", "dp"), "inner"),
            P(("groups", "expert", "dp"), None),
            P(("groups", "expert"), "inner", "dp"),
            P(("groups", "expert"), "inner", "dp"),
            P(("groups", "expert"), "dp", "inner"),
        ),
        check_vma=False,
    )
```

profile of v0, /device:TPU:0, one launch (start us, length us, event | category | flops | bytes accessed | tf_op | source)
XLA Modules:
  0.0 243.1 jit_solution(7060287537651137806)
XLA Ops:
  11.6 66.2 %all-gather.2.cloned.1.call-done = bf16[1024,1552]{0,1:T(8,128)(2,1)} async-done(((bf16[128,1552]{0,1:T(8,128)(2,1)}), bf16[1024,1552]{0,1:T(8,128)(2,1)}) %all-gather.2.cloned.1.call-update) | async-done | bytes 3178512 | tf_op jit(solution)/shard_map/all_gather | solution.py:43
  79.0 1.6 slice-done.2
  80.6 2.9 %copy.79 = bf16[1024,1536]{1,0:T(8,128)(2,1)} copy(bf16[1024,1536]{0,1:T(8,128)(2,1)S(1)} %slice-done.2) | data formatting | bytes 6291456 | tf_op jit(solution)/shard_map/reshape | solution.py:47
  83.6 8.2 %convert_bitcast_fusion = bf16[16,2,80,1536]{3,2,0,1:T(8,128)(2,1)} fusion(bf16[2,512,1536,1]{2,1,3,0:T(8,128)(2,1)} %bitcast.58, s32[2,16,512]{2,1,0:T(8,128)S(1)} %fusion.29), kind=kOutput, calls=%fused_computation.2 | convolution fusion | flops 4031774720 | bytes 11075584 | tf_op jit(solution)/shard_map/gest,gtd->egsd/dot_general | solution.py:48
  91.8 3.7 %copy.71 = bf16[16,2,80,1536]{3,2,1,0:T(8,128)(2,1)S(1)} copy(bf16[16,2,80,1536]{3,2,0,1:T(8,128)(2,1)} %convert_bitcast_fusion) | data formatting | bytes 15728640 | tf_op jit(solution)/shard_map/convert_element_type | solution.py:49
  95.5 6.9 %fusion.26 = bf16[16,160,192]{2,1,0:T(8,128)(2,1)S(1)} fusion(bf16[16,192,768]{2,1,0:T(8,128)(2,1)} %param.13, bf16[16,160,1536]{2,1,0:T(8,128)(2,1)S(1)} %bitcast.47), kind=kOutput, calls=%fused_computation.36 | convolution fusion | flops 755466240 | bytes 9633792 | tf_op jit(solution)/shard_map/jrd,jfd->jrf/dot_general | solution.py:57
  102.5 4.1 %fusion.23 = bf16[16,160,192]{2,1,0:T(8,128)(2,1)S(1)} fusion(bf16[16,768,192]{1,2,0:T(8,128)(2,1)} %param.12, bf16[16,160,1536]{2,1,0:T(8,128)(2,1)S(1)} %bitcast.48), kind=kOutput, calls=%fused_computation.35 | convolution fusion | flops 755466240 | bytes 9633792 | tf_op jit(solution)/shard_map/jrd,jdf->jrf/dot_general | solution.py:56
  106.6 4.0 %fusion.20 = bf16[16,160,192]{2,1,0:T(8,128)(2,1)S(1)} fusion(bf16[16,768,192]{1,2,0:T(8,128)(2,1)} %param.11, bf16[16,160,1536]{2,1,0:T(8,128)(2,1)S(1)} %bitcast.49), kind=kOutput, calls=%fused_computation.34 | convolution fusion | flops 755466240 | bytes 9633792 | tf_op jit(solution)/shard_map/jrd,jdf->jrf/dot_general | solution.py:55
  110.6 2.8 %pad_maximum_fusion = bf16[16,160,576]{2,1,0:T(8,128)(2,1)} fusion(bf16[16,160,192]{2,1,0:T(8,128)(2,1)S(1)} %fusion.26, bf16[16,160,192]{2,1,0:T(8,128)(2,1)S(1)} %fusion.23, bf16[16,160,192]{2,1,0:T(8,128)(2,1)S(1)} %fusion.20), kind=kLoop, calls=%fused_computation.14 | loop fusion | flops 8847360 | bytes 5898240 | tf_op jit(solution)/shard_map/concatenate | solution.py:53
  113.7 21.5 %all-reduce.2.cloned.1.call-done = bf16[16,160,576]{2,1,0:T(8,128)(2,1)} async-done(((bf16[16,160,576]{2,1,0:T(8,128)(2,1)}), bf16[16,160,576]{2,1,0:T(8,128)(2,1)}) %all-reduce.2.cloned.1.call-update) | async-done | bytes 2949136 | tf_op jit(solution)/shard_map/psum | solution.py:61
  135.2 2.6 %convert_element_type.75 = f32[16,160,576]{2,1,0:T(8,128)S(1)} convert(bf16[16,160,576]{2,1,0:T(8,128)(2,1)} %all-reduce.2.cloned.1.call-done) | non-fusion elementwise | flops 1474560 | bytes 8847360 | tf_op jit(solution)/shard_map/convert_element_type | solution.py:61
  137.8 2.7 %multiply_reduce_fusion.1 = (f32[16,160]{1,0:T(8,128)S(1)}, bf16[16,160,192]{2,1,0:T(8,128)(2,1)}) fusion(f32[16,160,576]{2,1,0:T(8,128)S(1)} %convert_element_type.75), kind=kLoop, calls=%fused_computation.19 | loop fusion | flops 4421120 | bytes 6891520 | tf_op jit(solution)/shard_map/reduce_sum | solution.py:66
  141.1 2.5 %select_reduce_fusion = (f32[2,16,80]{2,1,0:T(8,128)S(1)}, f32[2,16,512]{2,1,0:T(8,128)S(1)}) fusion(f32[2,16,512]{2,1,0:T(8,128)S(1)} %copy.68, s32[2,16,512]{2,1,0:T(8,128)S(1)} %fusion.29, f32[2,16,80]{2,1,0:T(8,128)S(1)} %copy.73), kind=kLoop, calls=%fused_computation.4 | loop fusion | flops 9156096 | bytes 217088 | tf_op jit(solution)/shard_map/reduce_sum | solution.py:30
  143.8 4.7 %multiply_convert_fusion.5 = (bf16[16,160,192]{2,1,0:T(8,128)(2,1)S(1)}, bf16[16,160,192]{2,1,0:T(8,128)(2,1)S(1)}) fusion(f32[16,160,576]{2,1,0:T(8,128)} %copy-done, f32[16,160]{1,0:T(8,128)S(1)} %mul.54), kind=kLoop, calls=%fused_computation.21 | loop fusion | flops 6881280 | bytes 7874560 | tf_op jit(solution)/shard_map/convert_element_type | solution.py:69
  148.6 3.6 %fusion.36 = f32[16,160,768]{2,1,0:T(8,128)S(1)} fusion(bf16[16,160,192]{2,1,0:T(8,128)(2,1)S(1)} %get-tuple-element.40, bf16[16,768,192]{1,2,0:T(8,128)(2,1)} %param.11), kind=kOutput, calls=%fused_computation.54 | convolution fusion | flops 754974720 | bytes 13565952 | tf_op jit(solution)/shard_map/jrf,jdf->jrd/dot_general | solution.py:70
  153.4 3.7 %bitcast_convert_fusion = bf16[2,512,768]{2,1,0:T(8,128)(2,1)} fusion(bf16[16,2,80,768]{3,2,1,0:T(8,128)(2,1)S(1)} %bitcast.57, s32[2,16,512]{2,1,0:T(8,128)S(1)} %fusion.29), kind=kOutput, calls=%fused_computation.15 | convolution fusion | flops 2015363072 | bytes 5570560 | tf_op jit(solution)/shard_map/gest,egsd->gtd/dot_general | solution.py:74
  157.1 2.6 %copy.75 = bf16[1024,768]{0,1:T(8,128)(2,1)} copy(bf16[1024,768]{1,0:T(8,128)(2,1)} %bitcast.59) | data formatting | bytes 3145728 | tf_op jit(solution)/shard_map/reshape | solution.py:79
  159.7 2.7 %pad_maximum_fusion.1 = bf16[1024,776]{0,1:T(8,128)(2,1)} fusion(bf16[1024,8]{0,1:T(8,128)(2,1)S(1)} %fusion.33, bf16[1024,768]{0,1:T(8,128)(2,1)} %copy.75), kind=kLoop, calls=%fused_computation.37 | loop fusion | flops 3178496 | bytes 3178496 | tf_op jit(solution)/shard_map/concatenate | solution.py:85
  162.4 3.7 %copy.80 = bf16[1024,776]{1,0:T(8,128)(2,1)} copy(bf16[1024,776]{0,1:T(8,128)(2,1)} %pad_maximum_fusion.1) | data formatting | bytes 3178496
  166.1 5.9 %convolution_convert_fusion.1 = bf16[16,768,192]{1,2,0:T(8,128)(2,1)} fusion(bf16[16,160,192]{2,1,0:T(8,128)(2,1)S(1)} %get-tuple-element.40, bf16[16,160,1536]{2,1,0:T(8,128)(2,1)} %bitcast.50), kind=kOutput, calls=%fused_computation.18 | convolution fusion | flops 757334016 | bytes 9633792 | tf_op jit(solution)/shard_map/jrd,jrf->jdf/dot_general | solution.py:90
  172.0 5.9 %convolution_convert_fusion = bf16[16,768,192]{1,2,0:T(8,128)(2,1)} fusion(bf16[16,160,192]{2,1,0:T(8,128)(2,1)S(1)} %get-tuple-element.39, bf16[16,160,1536]{2,1,0:T(8,128)(2,1)} %bitcast.51), kind=kOutput, calls=%fused_computation.17 | convolution fusion | flops 757334016 | bytes 9633792 | tf_op jit(solution)/shard_map/jrd,jrf->jdf/dot_general | solution.py:91
  178.0 3.5 %fusion.8 = bf16[16,192,768]{2,1,0:T(8,128)(2,1)} fusion(bf16[16,160,192]{2,1,0:T(8,128)(2,1)S(1)} %copy-done.2, f32[16,160]{1,0:T(8,128)S(1)} %mul.54, bf16[16,160,1536]{2,1,0:T(8,128)(2,1)S(1)} %bitcast.54), kind=kOutput, calls=%fused_computation.16 | convolution fusion | flops 763232256 | bytes 9977856 | tf_op jit(solution)/shard_map/jrf,jrd->jfd/dot_general | solution.py:93
  181.5 52.0 %reduce-scatter.4.cloned.1.call-done = bf16[128,776]{1,0:T(8,128)(2,1)} async-done(((bf16[1024,776]{1,0:T(8,128)(2,1)}), bf16[128,776]{1,0:T(8,128)(2,1)}) %reduce-scatter.4.cloned.1.call-update) | async-done | bytes 198672
  234.9 1.6 slice.48
  (45 shorter events, 9.4 us)
Async XLA Ops:
  7.2 70.7 %all-gather.2.cloned.1.call-start = ((), (), s32[]{:S(2)}) async-start(), calls=%async_computation.1 | async-start | bytes 3575808 | tf_op jit(solution)/shard_map/all_gather | solution.py:43
  11.6 123.6 %all-reduce.2.cloned.1.call-start = ((), (), s32[]{:S(2)}) async-start(), calls=%async_computation.2 | async-start | bytes 6553600 | tf_op jit(solution)/shard_map/psum | solution.py:61
  78.7 1.9 slice-start.2
  95.5 11.1 %copy-start.1 = (bf16[16,2,80,1536]{3,2,1,0:T(8,128)(2,1)}, bf16[16,2,80,1536]{3,2,1,0:T(8,128)(2,1)S(1)}, u32[]{:S(2)}) copy-start(bf16[16,2,80,1536]{3,2,1,0:T(8,128)(2,1)S(1)} %copy.71) | copy-start | bytes 23592964
  113.4 120.1 %reduce-scatter.4.cloned.1.call-start = ((), (), s32[]{:S(2)}) async-start(), calls=%async_computation.3 | async-start | bytes 2064384
  137.8 3.2 %copy-start = (f32[16,160,576]{2,1,0:T(8,128)}, f32[16,160,576]{2,1,0:T(8,128)S(1)}, u32[]{:S(2)}) copy-start(f32[16,160,576]{2,1,0:T(8,128)S(1)} %convert_element_type.75) | copy-start | bytes 17694724
  143.8 8.3 %slice-start.3 = ((s8[4718592]{0:T(1024)(128)(4,1)}), s8[4194304]{0:T(1024)(128)(4,1)S(1)}, s32[]{:S(2)}) async-start(s8[4718592]{0:T(1024)(128)(4,1)} %bitcast.55), calls=%async_computation.7 | async-start | bytes 8388608
  148.5 3.6 %slice-start.4 = ((s8[4718592]{0:T(1024)(128)(4,1)}), s8[524288]{0:T(1024)(128)(4,1)S(1)}, s32[]{:S(2)}) async-start(s8[4718592]{0:T(1024)(128)(4,1)} %bitcast.55), calls=%async_computation.8 | async-start | bytes 1048576
  166.1 11.9 %slice-start = ((s8[7864320]{0:T(1024)(128)(4,1)}), s8[4194304]{0:T(1024)(128)(4,1)S(1)}, s32[]{:S(2)}) async-start(s8[7864320]{0:T(1024)(128)(4,1)} %bitcast.52), calls=%async_computation.4 | async-start | bytes 8388608
  172.0 5.9 %slice-start.1 = ((s8[7864320]{0:T(1024)(128)(4,1)}), s8[3670016]{0:T(1024)(128)(4,1)S(1)}, s32[]{:S(2)}) async-start(s8[7864320]{0:T(1024)(128)(4,1)} %bitcast.52), calls=%async_computation.5 | async-start | bytes 7340032
  172.0 5.9 %copy-start.2 = (bf16[16,160,192]{2,1,0:T(8,128)(2,1)S(1)}, bf16[16,160,192]{2,1,0:T(8,128)(2,1)}, u32[]{:S(2)}) copy-start(bf16[16,160,192]{2,1,0:T(8,128)(2,1)} %get-tuple-element.38) | copy-start | bytes 2949124
Sparse Core Ops, SparseCore 0:
  11.7 66.1 all-gather.1
  113.5 21.6 all-reduce.1
  166.2 67.2 reduce-scatter.3
where the time goes:
time: 244 us; the launch traced here: 243 us
  waiting for transfers between devices  140 us (57%)
  matrix products  47.4 us (19%)
  other arithmetic  21.9 us (9%)
  local copies, waits for them, and re-layouts  19.9 us (8%)
  between operations  14 us (6%)
    all_gather x1, waiting for transfers between devices, on_device(): packed = lax.all_gather(packed, ('expert', 'dp'), axis=0, tiled=True)  66.2 us
    unnamed x4, waiting for transfers between devices  52 us
    psum x1, waiting for transfers between devices, on_device(): sums = lax.psum(parts, 'inner').astype(F32)  21.5 us
    dot_general x1, matrix products, on_device(): jnp.einsum('gest,gtd->egsd', picked, both, preferred_element_type=F32)  8.22 us
    dot_general x1, matrix products, on_device(): jnp.einsum('jrd,jfd->jrf', expert_grads, down_weight, preferred_element_t...  6.93 us
    unnamed x18, local copies, waits for them, and re-layouts  6.4 us
    dot_general x1, matrix products, on_device(): jnp.einsum('jrd,jrf->jdf', expert_rows, gate_back, preferred_element_type...  5.93 us
    dot_general x1, matrix products, on_device(): jnp.einsum('jrd,jrf->jdf', expert_rows, up_back, preferred_element_type=F32)  5.92 us
  transfers between devices with their start and end apart: 3, of which 3 were waited for; matrix products, arithmetic and copies ran while one was open for 6% of the time, Pallas kernels for 0%

commit v1 on v0

--- a/solution.py
+++ b/solution.py
@@ -5,6 +5,11 @@
 
 F32 = jnp.float32
 BF16 = jnp.bfloat16
+
+
+def gather_and_add(shard, axis):
+    parts = lax.all_gather(shard, axis)
+    return jnp.sum(parts, axis=0)
 
 
 def select_rows(packed, width, top_count, per_dev, block_rows, capacity):
@@ -58,7 +63,7 @@
         ],
         axis=2,
     ).astype(BF16)
-    sums = lax.psum(parts, "inner").astype(F32)
+    sums = gather_and_add(parts, "inner").astype(F32)
     gate, up, slope = (sums[..., :hid], sums[..., hid : 2 * hid], sums[..., 2 * hid :])
     sig = jax.nn.sigmoid(gate)
     act = gate * sig

time: 244 us -> 241 us (0.988)
  waiting for transfers between devices: 140 us -> 133 us
  other arithmetic: 21.9 us -> 25.4 us
    psum x1 -> x0, waiting for transfers between devices: 21.5 us -> none  [on_device(): sums = lax.psum(parts, 'inner').astype(F32)]
    all_gather x0 -> x1, waiting for transfers between devices: none -> 15.1 us  [gather_and_add(): parts = lax.all_gather(shard, axis)]
    reduce_sum x0 -> x1, other arithmetic: none -> 5.61 us  [gather_and_add(): return jnp.sum(parts, axis=0)]
where the time goes in v1:
time: 241 us; the launch traced here: 240 us
  waiting for transfers between devices  133 us (55%)
  matrix products  47.4 us (20%)
  other arithmetic  25.4 us (11%)
  local copies, waits for them, and re-layouts  19.9 us (8%)
  between operations  14 us (6%)
    all_gather x1, waiting for transfers between devices, on_device(): packed = lax.all_gather(packed, ('expert', 'dp'), axis=0, tiled=True)  66.2 us
    unnamed x4, waiting for transfers between devices  52.1 us
    all_gather x1, waiting for transfers between devices, gather_and_add(): parts = lax.all_gather(shard, axis)  15.1 us
    dot_general x1, matrix products, on_device(): jnp.einsum('gest,gtd->egsd', picked, both, preferred_element_type=F32)  8.22 us
    dot_general x1, matrix products, on_device(): jnp.einsum('jrd,jfd->jrf', expert_grads, down_weight, preferred_element_t...  6.93 us
    unnamed x18, local copies, waits for them, and re-layouts  6.4 us
    dot_general x1, matrix products, on_device(): jnp.einsum('jrd,jrf->jdf', expert_rows, gate_back, preferred_element_type...  5.93 us
    dot_general x1, matrix products, on_device(): jnp.einsum('jrd,jrf->jdf', expert_rows, up_back, preferred_element_type=F32)  5.92 us
  transfers between devices with their start and end apart: 3, of which 3 were waited for; matrix products, arithmetic and copies ran while one was open for 6% of the time, Pallas kernels for 0%

profile of v1, /device:TPU:0, one launch (start us, length us, event | category | flops | bytes accessed | tf_op | source)
XLA Modules:
  0.0 240.4 jit_solution(10522363143159193512)
XLA Ops:
  11.6 66.2 %all-gather.3.cloned.1.call-done = bf16[1024,1552]{0,1:T(8,128)(2,1)} async-done(((bf16[128,1552]{0,1:T(8,128)(2,1)}), bf16[1024,1552]{0,1:T(8,128)(2,1)}) %all-gather.3.cloned.1.call-update) | async-done | bytes 3178512 | tf_op jit(solution)/shard_map/all_gather | solution.py:48
  79.0 1.6 slice-done.2
  80.6 2.9 %copy.79 = bf16[1024,1536]{1,0:T(8,128)(2,1)} copy(bf16[1024,1536]{0,1:T(8,128)(2,1)S(1)} %slice-done.2) | data formatting | bytes 6291456 | tf_op jit(solution)/shard_map/reshape | solution.py:52
  83.6 8.2 %convert_bitcast_fusion = bf16[16,2,80,1536]{3,2,0,1:T(8,128)(2,1)} fusion(bf16[2,512,1536,1]{2,1,3,0:T(8,128)(2,1)} %bitcast.64, s32[2,16,512]{2,1,0:T(8,128)S(1)} %fusion.38), kind=kOutput, calls=%fused_computation.2 | convolution fusion | flops 4031774720 | bytes 11075584 | tf_op jit(solution)/shard_map/gest,gtd->egsd/dot_general | solution.py:53
  91.8 3.7 %copy.71 = bf16[16,2,80,1536]{3,2,1,0:T(8,128)(2,1)S(1)} copy(bf16[16,2,80,1536]{3,2,0,1:T(8,128)(2,1)} %convert_bitcast_fusion) | data formatting | bytes 15728640 | tf_op jit(solution)/shard_map/convert_element_type | solution.py:54
  95.5 6.9 %fusion.29 = bf16[1,16,160,192]{3,2,1,0:T(8,128)(2,1)S(1)} fusion(bf16[16,192,768]{2,1,0:T(8,128)(2,1)} %param.13, bf16[16,160,1536]{2,1,0:T(8,128)(2,1)S(1)} %bitcast.53), kind=kOutput, calls=%fused_computation.38 | convolution fusion | flops 755466240 | bytes 9633792 | tf_op jit(solution)/shard_map/jrd,jfd->jrf/dot_general | solution.py:62
  102.5 4.1 %fusion.32 = bf16[1,16,160,192]{3,2,1,0:T(8,128)(2,1)S(1)} fusion(bf16[16,768,192]{1,2,0:T(8,128)(2,1)} %param.12, bf16[16,160,1536]{2,1,0:T(8,128)(2,1)S(1)} %bitcast.54), kind=kOutput, calls=%fused_computation.39 | convolution fusion | flops 755466240 | bytes 9633792 | tf_op jit(solution)/shard_map/jrd,jdf->jrf/dot_general | solution.py:61
  106.6 4.0 %fusion.35 = bf16[1,16,160,192]{3,2,1,0:T(8,128)(2,1)S(1)} fusion(bf16[16,768,192]{1,2,0:T(8,128)(2,1)} %param.11, bf16[16,160,1536]{2,1,0:T(8,128)(2,1)S(1)} %bitcast.55), kind=kOutput, calls=%fused_computation.40 | convolution fusion | flops 755466240 | bytes 9633792 | tf_op jit(solution)/shard_map/jrd,jdf->jrf/dot_general | solution.py:60
  110.6 2.8 %pad_maximum_fusion = bf16[1,16,160,576]{3,2,1,0:T(8,128)(2,1)} fusion(bf16[1,16,160,192]{3,2,1,0:T(8,128)(2,1)S(1)} %fusion.29, bf16[1,16,160,192]{3,2,1,0:T(8,128)(2,1)S(1)} %fusion.32, bf16[1,16,160,192]{3,2,1,0:T(8,128)(2,1)S(1)} %fusion.35), kind=kLoop, calls=%fused_computation.14 | loop fusion | flops 8847360 | bytes 5898240 | tf_op jit(solution)/shard_map/concatenate | solution.py:58
  113.9 15.1 %all-gather.5.cloned.1.call-done = bf16[2,16,160,576]{3,2,1,0:T(8,128)(2,1)} async-done(((bf16[1,16,160,576]{3,2,1,0:T(8,128)(2,1)}), bf16[2,16,160,576]{3,2,1,0:T(8,128)(2,1)}) %all-gather.5.cloned.1.call-update) | async-done | bytes 5898256 | tf_op jit(solution)/shard_map/all_gather | solution.py:11
  128.9 5.6 %reduce_sum.59 = bf16[16,160,576]{2,1,0:T(8,128)(2,1)S(1)} reduce(bf16[2,16,160,576]{3,2,1,0:T(8,128)(2,1)} %all-gather.5.cloned.1.call-done, bf16[]{:T(256)} %constant.15.clone.1), dimensions={0}, to_apply=%region_3.4 | reduce | flops 1474560 | bytes 8847362 | tf_op jit(solution)/shard_map/reduce_sum | solution.py:12
  135.2 2.7 %multiply_reduce_fusion.1 = (f32[16,160]{1,0:T(8,128)S(1)}, bf16[16,160,192]{2,1,0:T(8,128)(2,1)}) fusion(f32[16,160,576]{2,1,0:T(8,128)S(1)} %convert_element_type.84), kind=kLoop, calls=%fused_computation.19 | loop fusion | flops 4421120 | bytes 6891520 | tf_op jit(solution)/shard_map/reduce_sum | solution.py:71
  138.4 2.3 select_reduce_fusion
  141.0 4.7 %multiply_convert_fusion.5 = (bf16[16,160,192]{2,1,0:T(8,128)(2,1)S(1)}, bf16[16,160,192]{2,1,0:T(8,128)(2,1)S(1)}) fusion(f32[16,160,576]{2,1,0:T(8,128)} %copy-done, f32[16,160]{1,0:T(8,128)S(1)} %mul.54), kind=kLoop, calls=%fused_computation.21 | loop fusion | flops 6881280 | bytes 7874560 | tf_op jit(solution)/shard_map/convert_element_type | solution.py:74
  145.8 3.6 %fusion.45 = f32[16,160,768]{2,1,0:T(8,128)S(1)} fusion(bf16[16,160,192]{2,1,0:T(8,128)(2,1)S(1)} %get-tuple-element.40, bf16[16,768,192]{1,2,0:T(8,128)(2,1)} %param.11), kind=kOutput, calls=%fused_computation.57 | convolution fusion | flops 754974720 | bytes 13565952 | tf_op jit(solution)/shard_map/jrf,jdf->jrd/dot_general | solution.py:75
  150.6 3.7 %bitcast_convert_fusion = bf16[2,512,768]{2,1,0:T(8,128)(2,1)} fusion(bf16[16,2,80,768]{3,2,1,0:T(8,128)(2,1)S(1)} %bitcast.63, s32[2,16,512]{2,1,0:T(8,128)S(1)} %fusion.38), kind=kOutput, calls=%fused_computation.15 | convolution fusion | flops 2015363072 | bytes 5570560 | tf_op jit(solution)/shard_map/gest,egsd->gtd/dot_general | solution.py:79
  154.3 2.6 %copy.75 = bf16[1024,768]{0,1:T(8,128)(2,1)} copy(bf16[1024,768]{1,0:T(8,128)(2,1)} %bitcast.65) | data formatting | bytes 3145728 | tf_op jit(solution)/shard_map/reshape | solution.py:84
  156.9 2.7 %pad_maximum_fusion.1 = bf16[1024,776]{0,1:T(8,128)(2,1)} fusion(bf16[1024,8]{0,1:T(8,128)(2,1)S(1)} %fusion.42, bf16[1024,768]{0,1:T(8,128)(2,1)} %copy.75), kind=kLoop, calls=%fused_computation.37 | loop fusion | flops 3178496 | bytes 3178496 | tf_op jit(solution)/shard_map/concatenate | solution.py:90
  159.6 3.7 %copy.80 = bf16[1024,776]{1,0:T(8,128)(2,1)} copy(bf16[1024,776]{0,1:T(8,128)(2,1)} %pad_maximum_fusion.1) | data formatting | bytes 3178496
  163.3 5.9 %convolution_convert_fusion.1 = bf16[16,768,192]{1,2,0:T(8,128)(2,1)} fusion(bf16[16,160,192]{2,1,0:T(8,128)(2,1)S(1)} %get-tuple-element.40, bf16[16,160,1536]{2,1,0:T(8,128)(2,1)} %bitcast.56), kind=kOutput, calls=%fused_computation.18 | convolution fusion | flops 757334016 | bytes 9633792 | tf_op jit(solution)/shard_map/jrd,jrf->jdf/dot_general | solution.py:95
  169.2 5.9 %convolution_convert_fusion = bf16[16,768,192]{1,2,0:T(8,128)(2,1)} fusion(bf16[16,160,192]{2,1,0:T(8,128)(2,1)S(1)} %get-tuple-element.39, bf16[16,160,1536]{2,1,0:T(8,128)(2,1)} %bitcast.57), kind=kOutput, calls=%fused_computation.17 | convolution fusion | flops 757334016 | bytes 9633792 | tf_op jit(solution)/shard_map/jrd,jrf->jdf/dot_general | solution.py:96
  175.2 3.5 %fusion.8 = bf16[16,192,768]{2,1,0:T(8,128)(2,1)} fusion(bf16[16,160,192]{2,1,0:T(8,128)(2,1)S(1)} %copy-done.2, f32[16,160]{1,0:T(8,128)S(1)} %mul.54, bf16[16,160,1536]{2,1,0:T(8,128)(2,1)S(1)} %bitcast.60), kind=kOutput, calls=%fused_computation.16 | convolution fusion | flops 763232256 | bytes 9977856 | tf_op jit(solution)/shard_map/jrf,jrd->jfd/dot_general | solution.py:98
  178.7 52.1 %reduce-scatter.4.cloned.1.call-done = bf16[128,776]{1,0:T(8,128)(2,1)} async-done(((bf16[1024,776]{1,0:T(8,128)(2,1)}), bf16[128,776]{1,0:T(8,128)(2,1)}) %reduce-scatter.4.cloned.1.call-update) | async-done | bytes 198672
  232.2 1.6 slice.48
  (46 shorter events, 10.2 us)
Async XLA Ops:
  7.2 70.7 %all-gather.3.cloned.1.call-start = ((), (), s32[]{:S(2)}) async-start(), calls=%async_computation.1 | async-start | bytes 3575808 | tf_op jit(solution)/shard_map/all_gather | solution.py:48
  11.6 117.3 %all-gather.5.cloned.1.call-start = ((), (), s32[]{:S(2)}) async-start(), calls=%async_computation.2 | async-start | bytes 9830400 | tf_op jit(solution)/shard_map/all_gather | solution.py:11
  78.7 1.9 slice-start.2
  95.5 11.1 %copy-start.1 = (bf16[16,2,80,1536]{3,2,1,0:T(8,128)(2,1)}, bf16[16,2,80,1536]{3,2,1,0:T(8,128)(2,1)S(1)}, u32[]{:S(2)}) copy-start(bf16[16,2,80,1536]{3,2,1,0:T(8,128)(2,1)S(1)} %copy.71) | copy-start | bytes 23592964
  113.4 117.3 %reduce-scatter.4.cloned.1.call-start = ((), (), s32[]{:S(2)}) async-start(), calls=%async_computation.3 | async-start | bytes 2064384
  135.2 3.2 %copy-start = (f32[16,160,576]{2,1,0:T(8,128)}, f32[16,160,576]{2,1,0:T(8,128)S(1)}, u32[]{:S(2)}) copy-start(f32[16,160,576]{2,1,0:T(8,128)S(1)} %convert_element_type.84) | copy-start | bytes 17694724
  141.0 8.3 %slice-start.3 = ((s8[4718592]{0:T(1024)(128)(4,1)}), s8[4194304]{0:T(1024)(128)(4,1)S(1)}, s32[]{:S(2)}) async-start(s8[4718592]{0:T(1024)(128)(4,1)} %bitcast.61), calls=%async_computation.7 | async-start | bytes 8388608
  145.7 3.6 %slice-start.4 = ((s8[4718592]{0:T(1024)(128)(4,1)}), s8[524288]{0:T(1024)(128)(4,1)S(1)}, s32[]{:S(2)}) async-start(s8[4718592]{0:T(1024)(128)(4,1)} %bitcast.61), calls=%async_computation.8 | async-start | bytes 1048576
  163.3 11.9 %slice-start = ((s8[7864320]{0:T(1024)(128)(4,1)}), s8[4194304]{0:T(1024)(128)(4,1)S(1)}, s32[]{:S(2)}) async-start(s8[7864320]{0:T(1024)(128)(4,1)} %bitcast.58), calls=%async_computation.4 | async-start | bytes 8388608
  169.2 5.9 %slice-start.1 = ((s8[7864320]{0:T(1024)(128)(4,1)}), s8[3670016]{0:T(1024)(128)(4,1)S(1)}, s32[]{:S(2)}) async-start(s8[7864320]{0:T(1024)(128)(4,1)} %bitcast.58), calls=%async_computation.5 | async-start | bytes 7340032
  169.2 5.9 %copy-start.2 = (bf16[16,160,192]{2,1,0:T(8,128)(2,1)S(1)}, bf16[16,160,192]{2,1,0:T(8,128)(2,1)}, u32[]{:S(2)}) copy-start(bf16[16,160,192]{2,1,0:T(8,128)(2,1)} %get-tuple-element.38) | copy-start | bytes 2949124
Sparse Core Ops, SparseCore 0:
  11.7 66.1 all-gather.2
  113.5 15.3 all-gather.4
  163.4 67.2 reduce-scatter.3
